TPU v7x, 32 devices: a whole 2x2x4 slice. The times are simulated.
32 devices in a mesh: layer: 2 (over y), facet: 16 (over z, x, core).
Axes of the slice: x: 2, y: 2, z: 4, core: 2. Of those that a mesh axis runs over, the one named last changes fastest.
Arguments:
- slabs: bfloat16 [2, 2, 64, 49152], P('layer', None, None, 'facet'), may hold values from -6 to 6
- window: float32 [49152], P('facet'), may hold values from 0.5 to 1.5
- density: int32 [2, 64, 8192], P('layer', None, 'facet'), may hold values from 0 to 7
- offsets: int32 [16], replicated, may hold values from 0 to 49151
Outputs:
- image_out: float32 [2, 64, 49152], P(None, 'layer', 'facet')
All inputs are finite; a program needn't handle non-finite values.
Results may differ from a plain program's by a relative error of at most 0.0052.
Values may be sent and summed in bfloat16 or wider, within the bound.
A program may use at most 64 MiB of HBM per device.

v0:
```python
import math

import jax
import jax.numpy as jnp
from jax import lax
from jax.sharding import PartitionSpec as P

CONTRIB = 128
SUB = 512


two_pi = 2.0 * math.pi


def mulmod(left_term, right_term, modulus):
    upper_part = right_term // 256
    lower_part = right_term % 256
    return jnp.mod(jnp.mod(left_term * upper_part, modulus) * 256 + left_term * lower_part, modulus)


def phase_parts(first_ints, places, image_width):
    phase_turns = mulmod(first_ints[:, None], places[None, :], image_width)
    phase_angle = phase_turns.astype(jnp.float32) * (-two_pi / image_width)
    return (jnp.cos(phase_angle), jnp.sin(phase_angle))


def embed_table(facet_count, facet_width, contrib_len, sub_len, image_width):
    sample_step = sub_len // contrib_len
    centres = jnp.arange(facet_count, dtype=jnp.int32) * facet_width + facet_width // 2
    sample_pos = jnp.arange(contrib_len, dtype=jnp.int32) * sample_step
    cell_ids = jnp.arange(sub_len, dtype=jnp.int32)
    spacing = cell_ids[None, :] - sample_pos[:, None]
    phase_turns = jnp.mod(spacing[None, :, :] * centres[:, None, None], image_width)
    phase_angle = phase_turns.astype(jnp.float32) * (-two_pi / image_width)
    scaled = spacing.astype(jnp.float32) / sample_step
    kernel = 1.0 / (1.0 + scaled * scaled)
    return jnp.stack([jnp.cos(phase_angle) * kernel, jnp.sin(phase_angle) * kernel], 1).astype(
        jnp.bfloat16
    )


def shards(slabs, window, density, offsets):
    facets = lax.axis_size("facet")
    position = lax.axis_index("facet")
    layer_slab = slabs[0]
    columns = layer_slab.shape[1]
    facet_width = layer_slab.shape[2]
    sample_step = SUB // CONTRIB
    image_width = facet_width * facets
    blocks = facets // 4
    block_ids = jnp.arange(blocks, dtype=jnp.int32)
    x_start = position * facet_width
    windowed = (layer_slab.astype(jnp.float32) * window[None, None, :]).astype(jnp.bfloat16)
    stacked = windowed.reshape(2 * columns, facet_width)
    places = x_start + jnp.arange(facet_width, dtype=jnp.int32)
    offset_cos, offset_sin = phase_parts(jnp.mod(offsets, image_width), places, image_width)
    step_cos, step_sin = phase_parts(
        sample_step * jnp.arange(CONTRIB, dtype=jnp.int32), places, image_width
    )

    def table_for(block_id):
        first_cos = lax.dynamic_slice_in_dim(offset_cos, block_id * 4, 4, 0)[:, None, :]
        first_sin = lax.dynamic_slice_in_dim(offset_sin, block_id * 4, 4, 0)[:, None, :]
        cos_part = first_cos * step_cos[None] - first_sin * step_sin[None]
        sin_part = first_cos * step_sin[None] + first_sin * step_cos[None]
        return jnp.stack([cos_part, sin_part], 1).astype(jnp.bfloat16)

    def encode_block(block_id):
        phase_table = table_for(block_id).reshape(8 * CONTRIB, facet_width)
        product = lax.dot_general(
            stacked, phase_table, (((1,), (1,)), ((), ())), preferred_element_type=jnp.float32
        )
        product = product.reshape(2, columns, 4, 2, CONTRIB)
        real_part = product[0, :, :, 0] - product[1, :, :, 1]
        imag_part = product[0, :, :, 1] + product[1, :, :, 0]
        return jnp.stack([real_part, imag_part], 0)

    pieces = lax.map(encode_block, block_ids)
    outgoing = (
        jnp.transpose(pieces, (0, 3, 1, 2, 4)).reshape(facets, 2, columns, CONTRIB)
        * facet_width ** (-0.5)
    ).astype(jnp.bfloat16)
    received = lax.all_to_all(outgoing, "facet", split_axis=0, concat_axis=0, tiled=True)
    embed_phase = embed_table(facets, facet_width, CONTRIB, SUB, image_width)
    raw_prod = lax.dot_general(
        received, embed_phase, (((0, 3), (0, 2)), ((), ())), preferred_element_type=jnp.float32
    )
    real_part = raw_prod[0, :, 0] - raw_prod[1, :, 1]
    imag_part = raw_prod[0, :, 1] + raw_prod[1, :, 0]
    counts = density[0]
    weights = jnp.where(
        counts > 0,
        1.0 / jnp.maximum(counts, 1).astype(jnp.float32),
        jnp.zeros(counts.shape, jnp.float32),
    )
    gridded = (
        jnp.stack([real_part, imag_part], 0) * weights[None] * (2 * facets) ** (-0.5)
    ).astype(jnp.bfloat16)
    raw_back = lax.dot_general(
        gridded, embed_phase, (((2,), (3,)), ((), ())), preferred_element_type=jnp.float32
    )
    real_back = raw_back[0, :, :, 0] + raw_back[1, :, :, 1]
    imag_back = raw_back[1, :, :, 0] - raw_back[0, :, :, 1]
    back_out = (jnp.stack([real_back, imag_back], 0) * 0.5).astype(jnp.bfloat16)
    returned = lax.all_to_all(back_out, "facet", split_axis=2, concat_axis=2, tiled=True)
    out_scale = (facets * CONTRIB) ** (-0.5)
    summed = lax.psum_scatter(
        returned.astype(jnp.float32).astype(jnp.bfloat16), "layer", scatter_dimension=1, tiled=True
    ).astype(jnp.float32)
    high_part = summed.astype(jnp.bfloat16)
    low_part = (summed - high_part.astype(jnp.float32)).astype(jnp.bfloat16)
    row_sets = [high_part, low_part]
    part_cols = row_sets[0].shape[1]

    def add_block(running, block_id):
        phase_table = table_for(block_id)
        terms = []
        for row_set in row_sets:
            part_rows = lax.dynamic_slice_in_dim(row_set, block_id * 4, 4, 2)
            terms.append(
                lax.dot_general(
                    part_rows,
                    phase_table,
                    (((2, 3), (0, 2)), ((), ())),
                    preferred_element_type=jnp.float32,
                )
            )
        combined = terms[0]
        for extra_term in terms[1:]:
            combined = combined + extra_term
        real_out = combined[0, :, 0] + combined[1, :, 1]
        imag_out = combined[1, :, 0] - combined[0, :, 1]
        return (running + jnp.stack([real_out, imag_out], 0), None)

    running, unused = lax.scan(
        add_block, jnp.zeros((2, part_cols, facet_width), jnp.float32), block_ids
    )
    image_out = running * window[None, None, :] * out_scale
    return image_out


def solution(mesh):
    placed = (P("layer", None, None, "facet"), P("facet"), P("layer", None, "facet"), P())
    return jax.shard_map(
        shards, mesh=mesh, in_specs=placed, out_specs=P(None, "layer", "facet"), check_vma=False
    )
```

profile of v0, /device:TPU:1, one launch (start us, length us, event | category | flops | bytes accessed | tf_op | source)
XLA Modules:
  0.0 194.8 jit_solution(16043260251125847678)
XLA Ops:
  7.2 1.3 fusion.48
  9.5 55.1 %while.25 = (s32[]{:T(128)}, f32[4,2,64,4,128]{4,3,2,1,0:T(4,128)S(1)}, s32[4]{0:T(128)S(1)}, f32[16,3072]{1,0:T(8,128)S(1)}, f32[16,3072]{1,0:T(8,128)S(1)}, /*...) while((s32[]{:T(128)}, ...), condition=%wide.region_1.2_spmd.clone.clone, body=%wide.region_0.1_spmd.clone.clone.sunk | while | flops 828243968 | bytes 37020348 | solution.py:78
  10.7 7.3 %fusion.98 = (f32[128,3072]{1,0:T(8,128)S(1)}, f32[128,3072]{1,0:T(8,128)S(1)}) fusion(s32[3072]{0:T(1024)S(1)} %get-tuple-element.527, s32[3072]{0:T(1024)S(1)} %get-tuple-element.526, s32[128]{0:T(128)S(1)} %get-tuple-element.528), kind=kLoop, calls=%fused_computation.20.clone.1 | loop fusion | flops 7077888 | bytes 3170816 | tf_op jit(solution)/shard_map/cos | solution.py:24
  18.0 1.7 subtract_convert_fusion.5
  20.3 1.8 convolution_bitcast_fusion.2
  24.4 7.3 %fusion.98 = (f32[128,3072]{1,0:T(8,128)S(1)}, f32[128,3072]{1,0:T(8,128)S(1)}) fusion(s32[3072]{0:T(1024)S(1)} %get-tuple-element.527, s32[3072]{0:T(1024)S(1)} %get-tuple-element.526, s32[128]{0:T(128)S(1)} %get-tuple-element.528), kind=kLoop, calls=%fused_computation.20.clone.1 | loop fusion | flops 7077888 | bytes 3170816 | tf_op jit(solution)/shard_map/cos | solution.py:24
  31.7 1.7 subtract_convert_fusion.5
  34.1 1.8 convolution_bitcast_fusion.2
  38.2 7.3 %fusion.98 = (f32[128,3072]{1,0:T(8,128)S(1)}, f32[128,3072]{1,0:T(8,128)S(1)}) fusion(s32[3072]{0:T(1024)S(1)} %get-tuple-element.527, s32[3072]{0:T(1024)S(1)} %get-tuple-element.526, s32[128]{0:T(128)S(1)} %get-tuple-element.528), kind=kLoop, calls=%fused_computation.20.clone.1 | loop fusion | flops 7077888 | bytes 3170816 | tf_op jit(solution)/shard_map/cos | solution.py:24
  45.4 1.7 subtract_convert_fusion.5
  47.8 1.8 convolution_bitcast_fusion.2
  51.9 7.3 %fusion.98 = (f32[128,3072]{1,0:T(8,128)S(1)}, f32[128,3072]{1,0:T(8,128)S(1)}) fusion(s32[3072]{0:T(1024)S(1)} %get-tuple-element.527, s32[3072]{0:T(1024)S(1)} %get-tuple-element.526, s32[128]{0:T(128)S(1)} %get-tuple-element.528), kind=kLoop, calls=%fused_computation.20.clone.1 | loop fusion | flops 7077888 | bytes 3170816 | tf_op jit(solution)/shard_map/cos | solution.py:24
  59.2 1.7 subtract_convert_fusion.5
  61.5 1.8 convolution_bitcast_fusion.2
  65.8 7.3 %all-to-all-start = ((bf16[16,2,64,128]{3,2,1,0:T(8,128)(2,1)}), bf16[16,2,64,128]{3,2,1,0:T(8,128)(2,1)S(1)}, u32[]{:S(2)}, u32[]{:S(2)}) async-start(bf16[16,2,64,128]{3,2,1,0:T(8,128)(2,1)} %bitcast.2), calls=%async_computation | async-start | bytes 1048576 | tf_op jit(solution)/shard_map/all_to_all | solution.py:83
  73.5 18.9 %multiply_convert_fusion.1 = (bf16[16,1,128,512]{3,2,0,1:T(8,128)(2,1)S(1)}, bf16[16,1,128,512]{3,2,0,1:T(8,128)(2,1)}) fusion(f32[128,512]{1,0:T(8,128)S(1)} %add_divide_fusion, s32[16]{0:T(128)S(1)} %multiply_add_fusion, s32[128,512]{1,0:T(8,128)S(1)} %iota_subtract_fusion), kind=kLoop, calls=%fused_computation.71 | loop fusion | flops 13631488 | bytes 4718656 | tf_op jit(solution)/shard_map/convert.5
  92.4 2.4 %fusion.49 = f32[2,64,2,512]{3,1,2,0:T(8,128)S(1)} fusion(bf16[16,1,128,512]{3,2,0,1:T(8,128)(2,1)} %get-tuple-element.333, bf16[16,1,128,512]{3,2,0,1:T(8,128)(2,1)S(1)} %get-tuple-element.332, bf16[16,2,64,128]{3,2,1,0:T(8,128)(2,1)S(1)} %all-to-all-done), kind=kOutput, calls=%fused_computation.78 | convolution fusion | flops 545259520 | bytes 5242880 | tf_op jit(solution)/shard_map/dot_general | solution.py:85
  94.9 1.5 fusion.40
  96.7 19.9 %all_to_all.10 = bf16[2,64,16,128]{3,1,0,2:T(8,128)(2,1)} all-to-all(bf16[2,64,16,128]{3,1,0,2:T(8,128)(2,1)S(1)} %copy.28), channel_id=1, replica_groups=mesh['layer'=2,'facet'=16] {'facet'}, dimensions={2} | all-to-all | bytes 1048576 | tf_op jit(solution)/shard_map/all_to_all | solution.py:105
  116.6 13.9 %reduce-scatter.2.cloned.1.call-done = bf16[2,32,16,128]{3,1,0,2:T(8,128)(2,1)} async-done(((bf16[2,64,16,128]{3,1,0,2:T(8,128)(2,1)}), bf16[2,32,16,128]{3,1,0,2:T(8,128)(2,1)}) %reduce-scatter.2.cloned.1.call-update) | async-done | bytes 262160 | tf_op jit(solution)/shard_map/reduce_scatter | solution.py:107
  131.5 55.4 %while.26 = (s32[]{:T(128)}, f32[2,32,3072]{2,1,0:T(8,128)S(1)}, s32[4]{0:T(128)S(1)}, bf16[2,32,16,128]{3,1,0,2:T(8,128)(2,1)}, f32[16,3072]{1,0:T(8,128)S(1)},...) while((s32[]{:T(128)}, f32[2,32,3072]{2,1,0:T(8,128)S(1)}, ...), condition=%wide.region_4.5_spmd.clone.clone.clone, body=%wide.region_3.4_spmd.clone.clone.clone.sunk | while | flops 851312640 | bytes 35316432 | solution.py:135
  132.7 7.3 %fusion.101 = (f32[128,3072]{1,0:T(8,128)S(1)}, f32[128,3072]{1,0:T(8,128)S(1)}) fusion(s32[3072]{0:T(1024)S(1)} %get-tuple-element.569, s32[3072]{0:T(1024)S(1)} %get-tuple-element.568, s32[128]{0:T(128)S(1)} %get-tuple-element.570), kind=kLoop, calls=%fused_computation.48.clone.1 | loop fusion | flops 7077888 | bytes 3170816 | tf_op jit(solution)/shard_map/cos | solution.py:24
  140.0 1.7 subtract_convert_fusion.6
  143.8 1.2 fusion.103
  146.6 7.3 %fusion.101 = (f32[128,3072]{1,0:T(8,128)S(1)}, f32[128,3072]{1,0:T(8,128)S(1)}) fusion(s32[3072]{0:T(1024)S(1)} %get-tuple-element.569, s32[3072]{0:T(1024)S(1)} %get-tuple-element.568, s32[128]{0:T(128)S(1)} %get-tuple-element.570), kind=kLoop, calls=%fused_computation.48.clone.1 | loop fusion | flops 7077888 | bytes 3170816 | tf_op jit(solution)/shard_map/cos | solution.py:24
  153.9 1.7 subtract_convert_fusion.6
  157.7 1.2 fusion.103
  160.4 7.3 %fusion.101 = (f32[128,3072]{1,0:T(8,128)S(1)}, f32[128,3072]{1,0:T(8,128)S(1)}) fusion(s32[3072]{0:T(1024)S(1)} %get-tuple-element.569, s32[3072]{0:T(1024)S(1)} %get-tuple-element.568, s32[128]{0:T(128)S(1)} %get-tuple-element.570), kind=kLoop, calls=%fused_computation.48.clone.1 | loop fusion | flops 7077888 | bytes 3170816 | tf_op jit(solution)/shard_map/cos | solution.py:24
  167.7 1.7 subtract_convert_fusion.6
  171.5 1.2 fusion.103
  174.3 7.3 %fusion.101 = (f32[128,3072]{1,0:T(8,128)S(1)}, f32[128,3072]{1,0:T(8,128)S(1)}) fusion(s32[3072]{0:T(1024)S(1)} %get-tuple-element.569, s32[3072]{0:T(1024)S(1)} %get-tuple-element.568, s32[128]{0:T(128)S(1)} %get-tuple-element.570), kind=kLoop, calls=%fused_computation.48.clone.1 | loop fusion | flops 7077888 | bytes 3170816 | tf_op jit(solution)/shard_map/cos | solution.py:24
  181.6 1.7 subtract_convert_fusion.6
  (87 shorter events, 27.8 us)
Async XLA Ops:
  64.6 8.6 %copy-start.1 = (s32[1,64,512]{2,1,0:T(8,128)S(1)}, s32[1,64,512]{2,1,0:T(8,128)}, u32[]{:S(2)}) copy-start(s32[1,64,512]{2,1,0:T(8,128)} %param.10) | copy-start | bytes 393220
  65.8 26.5 %all-to-all-start = ((bf16[16,2,64,128]{3,2,1,0:T(8,128)(2,1)}), bf16[16,2,64,128]{3,2,1,0:T(8,128)(2,1)S(1)}, u32[]{:S(2)}, u32[]{:S(2)}) async-start(bf16[16,2,64,128]{3,2,1,0:T(8,128)(2,1)} %bitcast.2), calls=%async_computation | async-start | bytes 1048576 | tf_op jit(solution)/shard_map/all_to_all | solution.py:83
  73.1 57.4 %reduce-scatter.2.cloned.1.call-start = ((), (), s32[]{:S(2)}) async-start(), calls=%async_computation.3 | async-start | bytes 786432 | tf_op jit(solution)/shard_map/reduce_scatter | solution.py:107
  92.4 2.5 %copy-start = (bf16[16,1,128,512]{3,2,0,1:T(8,128)(2,1)S(1)}, bf16[16,1,128,512]{3,2,0,1:T(8,128)(2,1)}, u32[]{:S(2)}) copy-start(bf16[16,1,128,512]{3,2,0,1:T(8,128)(2,1)} %get-tuple-element.333) | copy-start | bytes 6291460
  131.5 55.5 %copy-start.2 = (f32[3072]{0:T(1024)S(1)}, f32[3072]{0:T(1024)}, u32[]{:S(2)}) copy-start(f32[3072]{0:T(1024)} %param.9) | copy-start | bytes 36868
Sparse Core Ops, SparseCore 0:
  116.7 13.7 reduce-scatter.1
where the time goes:
time: 196 us; the launch traced here: 195 us
  other arithmetic  102 us (52%)
  matrix products  20.7 us (11%)
  blocking collectives  19.9 us (10%)
  waiting for transfers between devices  13.9 us (7%)
  between operations  13.6 us (7%)
  local copies, waits for them, and re-layouts  11.9 us (6%)
  starting transfers between devices  7.34 us (4%)
  loops' own time  5.35 us (3%)
    cos x8, other arithmetic, phase_parts(): return (jnp.cos(phase_angle), jnp.sin(phase_angle))  58.1 us
    another operation x9, other arithmetic  32.9 us
    all_to_all x1, blocking collectives, shards(): lax.all_to_all(back_out, 'facet', split_axis=2, concat_axis=2, tiled=True)  19.9 us
    reduce_scatter x1, waiting for transfers between devices, shards(): lax.psum_scatter(returned.astype(jnp.float32).astype(jnp.bfloat16), 'laye...  13.9 us
    dot_general x8, matrix products, add_block(): lax.dot_general(part_rows, phase_table, (((2, 3), (0, 2)), ((), ())), pre...  9.64 us
    all_to_all x1, starting transfers between devices, shards(): lax.all_to_all(outgoing, 'facet', split_axis=0, concat_axis=0, tiled=True)  7.31 us
    dot_general x4, matrix products, encode_block(): lax.dot_general(stacked, phase_table, (((1,), (1,)), ((), ())), preferred...  7.15 us
    dynamic_slice x8, local copies, waits for them, and re-layouts, shards(): pieces = lax.map(encode_block, block_ids)  4.69 us
  transfers between devices with their start and end apart: 2, of which 1 were waited for; matrix products, arithmetic and copies ran while one was open for 10% of the time, Pallas kernels for 0%

commit v1 on v0

v1 whole, which is shorter than its diff:
```python
import functools
import math

import jax
import jax.numpy as jnp
from jax import lax
from jax.experimental import pallas as pl
from jax.experimental.pallas import tpu as pltpu
from jax.sharding import PartitionSpec as P

CONTRIB = 128
SUB = 512
GROUP = 4
CHUNK = 512
ROWS = 256
STEP = SUB // CONTRIB

MESH = pl.DeviceIdType.MESH


def sincos(turns, period):
    quarter = jnp.floor(turns.astype(jnp.float32) * (4.0 / period) + 0.5).astype(jnp.int32)
    rest = 4 * turns - quarter * period
    y = rest.astype(jnp.float32) * (0.5 * math.pi / period)
    z = y * y
    s = y + y * z * (-1.0 / 6 + z * (1.0 / 120 + z * (-1.0 / 5040 + z * (1.0 / 362880))))
    c = 1.0 + z * (-0.5 + z * (1.0 / 24 + z * (-1.0 / 720 + z * (1.0 / 40320))))
    odd = (quarter & 1) == 1
    cos_abs = jnp.where(odd, s, c)
    sin_abs = jnp.where(odd, c, s)
    cos_part = jnp.where(((quarter + 1) & 2) == 2, -cos_abs, cos_abs)
    sin_part = jnp.where((quarter & 2) == 2, -sin_abs, sin_abs)
    return cos_part, sin_part


def remainder(value, period):
    return value - jnp.floor(value.astype(jnp.float32) * (1.0 / period)).astype(jnp.int32) * period


def kernel(
    layers, facets, cols, width,
    slab_ref, window_ref, density_ref, offset_ref,
    out_ref,
    wind, ca, sa, table, modulated, acc,
    send1, recv1, embed, kr, ki, rr, ri, raw,
    send2, recv2,
    ssem1, rsem1, ssem2, rsem2,
):
    layer = lax.axis_index("layer")
    me = lax.axis_index("facet")
    rank = layer * facets + me
    total = layers * facets
    image = facets * width
    groups = facets // GROUP
    part = cols // layers

    barrier = pltpu.get_barrier_semaphore()

    def greet(step, carry):
        other = lax.rem(rank + step, total)
        pl.semaphore_signal(
            barrier, inc=1,
            device_id=(other // facets, lax.rem(other, facets)), device_id_type=MESH,
        )
        return carry

    lax.fori_loop(1, total, greet, 0)

    window = window_ref[...]
    for p in range(2):
        wind[p * cols:(p + 1) * cols, :] = (
            (slab_ref[0, p].astype(jnp.float32) * window).astype(jnp.bfloat16).astype(jnp.float32)
        )

    offs = offset_ref[...]
    start = remainder(offs * me, facets) * width
    cell = lax.broadcasted_iota(jnp.int32, (facets, width), 1)
    turns = start + remainder(offs * cell, image)
    cos_a, sin_a = sincos(turns, image)
    ca[...] = cos_a
    sa[...] = sin_a

    lane = lax.broadcasted_iota(jnp.int32, (ROWS, CONTRIB), 1) * STEP
    row = lax.broadcasted_iota(jnp.int32, (ROWS, CONTRIB), 0)
    base_c, base_s = sincos(remainder(lane * me, facets) * width + remainder(lane * row, image), image)
    small = lax.broadcasted_iota(jnp.int32, (8, CONTRIB), 1) * STEP
    for k in range(width // ROWS):
        rot_c, rot_s = sincos(remainder(small * (ROWS * k), image), image)
        rot_c = rot_c[0:1]
        rot_s = rot_s[0:1]
        table[k * ROWS:(k + 1) * ROWS, 0:CONTRIB] = (base_c * rot_c - base_s * rot_s).astype(jnp.bfloat16)
        table[k * ROWS:(k + 1) * ROWS, CONTRIB:2 * CONTRIB] = (
            base_c * rot_s + base_s * rot_c
        ).astype(jnp.bfloat16)

    half = me // (facets // 2)
    half_groups = groups // 2
    scale1 = width ** -0.5

    def encode(step, carry):
        g = lax.rem((1 - half) * half_groups + step, groups)
        for k in range(width // CHUNK):
            xs = slice(k * CHUNK, (k + 1) * CHUNK)
            for t in range(GROUP):
                s = g * GROUP + t
                c_row = ca[pl.ds(s, 1), xs]
                s_row = sa[pl.ds(s, 1), xs]
                wr = wind[0:cols, xs]
                wi = wind[cols:2 * cols, xs]
                lo = t * 2 * cols
                modulated[k % 2, lo:lo + cols, :] = (wr * c_row + wi * s_row).astype(jnp.bfloat16)
                modulated[k % 2, lo + cols:lo + 2 * cols, :] = (wi * c_row - wr * s_row).astype(jnp.bfloat16)
            prod = jnp.dot(modulated[k % 2], table[xs, :], preferred_element_type=jnp.float32)
            if k == 0:
                acc[...] = prod
            else:
                acc[...] += prod
        for t in range(GROUP):
            lo = t * 2 * cols
            pr = acc[lo:lo + cols, :]
            pi = acc[lo + cols:lo + 2 * cols, :]
            real = pr[:, :CONTRIB] + pi[:, CONTRIB:]
            imag = pi[:, :CONTRIB] - pr[:, CONTRIB:]
            send1[g * GROUP + t, 0:cols, :] = (real * scale1).astype(jnp.bfloat16)
            send1[g * GROUP + t, cols:2 * cols, :] = (imag * scale1).astype(jnp.bfloat16)

        @pl.when(step == 0)
        def _():
            pl.semaphore_wait(barrier, total - 1)

        for t in range(GROUP):
            s = g * GROUP + t

            @pl.when(s != me)
            def _():
                pltpu.make_async_remote_copy(
                    src_ref=send1.at[s], dst_ref=recv1.at[me],
                    send_sem=ssem1.at[s], recv_sem=rsem1.at[me],
                    device_id=(layer, s), device_id_type=MESH,
                ).start()

            @pl.when(s == me)
            def _():
                recv1[s] = send1[s]

        return carry

    lax.fori_loop(0, groups, encode, 0)

    spacing = lax.broadcasted_iota(jnp.int32, (CONTRIB, SUB), 1) - STEP * lax.broadcasted_iota(
        jnp.int32, (CONTRIB, SUB), 0
    )
    scaled = spacing.astype(jnp.float32) * (1.0 / STEP)
    weight_k = 1.0 / (1.0 + scaled * scaled)
    c0, s0 = sincos(spacing, 2 * facets)
    kr[...] = c0 * weight_k
    ki[...] = s0 * weight_k
    c1, s1 = sincos(spacing, facets)
    rr[...] = c1
    ri[...] = s1

    def make_embed(f, carry):
        r = kr[...]
        i = ki[...]
        lo = pl.multiple_of(f * CONTRIB, CONTRIB)
        embed[pl.ds(lo, CONTRIB), 0:SUB] = r.astype(jnp.bfloat16)
        embed[pl.ds(lo, CONTRIB), SUB:2 * SUB] = (-i).astype(jnp.bfloat16)
        a = rr[...]
        b = ri[...]
        kr[...] = r * a - i * b
        ki[...] = r * b + i * a
        return carry

    lax.fori_loop(0, facets, make_embed, 0)
    raw[...] = jnp.zeros_like(raw)

    def gather(step, carry):
        g = lax.rem(half * half_groups + step, groups)
        for t in range(GROUP):
            f = g * GROUP + t

            @pl.when(f != me)
            def _():
                pltpu.make_async_remote_copy(
                    src_ref=send1.at[f], dst_ref=recv1.at[f],
                    send_sem=ssem1.at[f], recv_sem=rsem1.at[f],
                    device_id=(layer, f), device_id_type=MESH,
                ).wait()

        lhs = jnp.concatenate([recv1[g * GROUP + t] for t in range(GROUP)], axis=1)
        lo = pl.multiple_of(g * GROUP * CONTRIB, GROUP * CONTRIB)
        raw[...] += jnp.dot(
            lhs, embed[pl.ds(lo, GROUP * CONTRIB), :], preferred_element_type=jnp.float32
        )
        return carry

    lax.fori_loop(0, groups, gather, 0)

    counts = density_ref[0]
    weights = jnp.where(
        counts > 0, 1.0 / jnp.maximum(counts, 1).astype(jnp.float32), 0.0
    )
    sub_scale = (2 * facets) ** -0.5
    raw_r = raw[0:cols, 0:SUB] - raw[cols:2 * cols, SUB:2 * SUB]
    raw_i = raw[0:cols, SUB:2 * SUB] + raw[cols:2 * cols, 0:SUB]
    gridded = jnp.concatenate(
        [
            (raw_r * weights * sub_scale).astype(jnp.bfloat16),
            (raw_i * weights * sub_scale).astype(jnp.bfloat16),
        ],
        axis=0,
    )
    dims = (((1,), (1,)), ((), ()))

    def scatter(step, carry):
        g = lax.rem((1 - half) * half_groups + step, groups)
        lo = pl.multiple_of(g * GROUP * CONTRIB, GROUP * CONTRIB)
        er = embed[pl.ds(lo, GROUP * CONTRIB), 0:SUB]
        ei = embed[pl.ds(lo, GROUP * CONTRIB), SUB:2 * SUB]
        pr = lax.dot_general(gridded, er, dims, preferred_element_type=jnp.float32)
        pi = lax.dot_general(gridded, ei, dims, preferred_element_type=jnp.float32)
        real = ((pr[0:cols] + pi[cols:2 * cols]) * 0.5).astype(jnp.bfloat16)
        imag = ((pr[cols:2 * cols] - pi[0:cols]) * 0.5).astype(jnp.bfloat16)
        for t in range(GROUP):
            f = g * GROUP + t
            js = slice(t * CONTRIB, (t + 1) * CONTRIB)
            for l in range(layers):
                send2[f, l, 0] = real[l * part:(l + 1) * part, js]
                send2[f, l, 1] = imag[l * part:(l + 1) * part, js]
        for t in range(GROUP):
            f = g * GROUP + t
            for l in range(layers):
                own = jnp.logical_and(f == me, layer == l)

                @pl.when(jnp.logical_not(own))
                def _():
                    pltpu.make_async_remote_copy(
                        src_ref=send2.at[f, l], dst_ref=recv2.at[layer, me],
                        send_sem=ssem2.at[l, f], recv_sem=rsem2.at[layer, me],
                        device_id=(l, f), device_id_type=MESH,
                    ).start()

                @pl.when(own)
                def _():
                    recv2[layer, me] = send2[f, l]

        return carry

    lax.fori_loop(0, groups, scatter, 0)

    out_ref[...] = jnp.zeros_like(out_ref)

    def adjoint(step, carry):
        g = lax.rem(half * half_groups + step, groups)
        tops = []
        for t in range(GROUP):
            s = g * GROUP + t
            for l in range(layers):
                own = jnp.logical_and(s == me, layer == l)

                @pl.when(jnp.logical_not(own))
                def _():
                    pltpu.make_async_remote_copy(
                        src_ref=send2.at[s, l], dst_ref=recv2.at[l, s],
                        send_sem=ssem2.at[l, s], recv_sem=rsem2.at[l, s],
                        device_id=(l, s), device_id_type=MESH,
                    ).wait()

        for t in range(GROUP):
            s = g * GROUP + t
            br = recv2[0, s, 0].astype(jnp.float32)
            bi = recv2[0, s, 1].astype(jnp.float32)
            for l in range(1, layers):
                br = br + recv2[l, s, 0].astype(jnp.float32)
                bi = bi + recv2[l, s, 1].astype(jnp.float32)
            tops.append(jnp.concatenate([br, -bi], axis=1))
            tops.append(jnp.concatenate([bi, br], axis=1))
        lhs = jnp.concatenate(tops, axis=0).astype(jnp.bfloat16)
        for k in range(width // CHUNK):
            xs = slice(k * CHUNK, (k + 1) * CHUNK)
            prod = lax.dot_general(lhs, table[xs, :], dims, preferred_element_type=jnp.float32)
            out_r = out_ref[0, :, xs]
            out_i = out_ref[1, :, xs]
            for t in range(GROUP):
                s = g * GROUP + t
                c_row = ca[pl.ds(s, 1), xs]
                s_row = sa[pl.ds(s, 1), xs]
                gr = prod[(2 * t) * part:(2 * t + 1) * part]
                gi = prod[(2 * t + 1) * part:(2 * t + 2) * part]
                out_r = out_r + (c_row * gr - s_row * gi)
                out_i = out_i + (c_row * gi + s_row * gr)
            out_ref[0, :, xs] = out_r
            out_ref[1, :, xs] = out_i
        return carry

    lax.fori_loop(0, groups, adjoint, 0)


def shards(slabs, window, density, offsets):
    facets = lax.axis_size("facet")
    layers = lax.axis_size("layer")
    cols = slabs.shape[2]
    width = slabs.shape[3]
    part = cols // layers
    f32, bf16 = jnp.float32, jnp.bfloat16
    summed = pl.pallas_call(
        functools.partial(kernel, layers, facets, cols, width),
        out_shape=jax.ShapeDtypeStruct((2, part, width), f32),
        in_specs=[pl.BlockSpec(memory_space=pltpu.VMEM)] * 4,
        out_specs=pl.BlockSpec(memory_space=pltpu.VMEM),
        scratch_shapes=[
            pltpu.VMEM((2 * cols, width), f32),
            pltpu.VMEM((facets, width), f32),
            pltpu.VMEM((facets, width), f32),
            pltpu.VMEM((width, 2 * CONTRIB), bf16),
            pltpu.VMEM((2, GROUP * 2 * cols, CHUNK), bf16),
            pltpu.VMEM((GROUP * 2 * cols, 2 * CONTRIB), f32),
            pltpu.VMEM((facets, 2 * cols, CONTRIB), bf16),
            pltpu.VMEM((facets, 2 * cols, CONTRIB), bf16),
            pltpu.VMEM((facets * CONTRIB, 2 * SUB), bf16),
            pltpu.VMEM((CONTRIB, SUB), f32),
            pltpu.VMEM((CONTRIB, SUB), f32),
            pltpu.VMEM((CONTRIB, SUB), f32),
            pltpu.VMEM((CONTRIB, SUB), f32),
            pltpu.VMEM((2 * cols, 2 * SUB), f32),
            pltpu.VMEM((facets, layers, 2, part, CONTRIB), bf16),
            pltpu.VMEM((layers, facets, 2, part, CONTRIB), bf16),
            pltpu.SemaphoreType.DMA((facets,)),
            pltpu.SemaphoreType.DMA((facets,)),
            pltpu.SemaphoreType.DMA((layers, facets)),
            pltpu.SemaphoreType.DMA((layers, facets)),
        ],
        compiler_params=pltpu.CompilerParams(
            collective_id=0, has_side_effects=True, vmem_limit_bytes=56 * 1024 * 1024
        ),
    )(slabs, window[None, :], density, offsets[:, None])
    return summed * (window[None, None, :] * (facets * CONTRIB) ** -0.5)


def solution(mesh):
    placed = (P("layer", None, None, "facet"), P("facet"), P("layer", None, "facet"), P())
    return jax.shard_map(
        shards, mesh=mesh, in_specs=placed, out_specs=P(None, "layer", "facet"), check_vma=False
    )
```

time: 196 us -> 38.1 us (0.19)
  the two profiles are of different devices: /device:TPU:1 before, /device:TPU:9 now
where the time goes in v1:
time: 38.1 us; the launch traced here: 37.9 us
  Pallas kernels  34.5 us (91%)
  other arithmetic  2.07 us (5%)
  local copies, waits for them, and re-layouts  1.34 us (4%)
    pallas_call x1, Pallas kernels, shards(): pl.pallas_call(functools.partial(kernel, layers, facets, cols, width), ou...  34.5 us
    mul x2, other arithmetic, shards(): return summed * (window[None, None, :] * (facets * CONTRIB) ** (-0.5))  2.07 us

profile of v1, /device:TPU:9, one launch (start us, length us, event | category | flops | bytes accessed | tf_op | source)
XLA Modules:
  0.0 37.9 jit_solution(804988929213090752)
XLA Ops:
  0.0 0.0 copy-start.1
  0.0 0.7 %copy-done.1 = s32[16]{0:T(128)S(1)} copy-done((s32[16]{0:T(128)S(1)}, s32[16]{0:T(128)}, u32[]{:S(2)}) %copy-start.1) | copy-done | bytes 88
  0.7 0.7 %copy.5.offset_ref = s32[16,1]{1,0:T(8,128)} copy(s32[16,1]{0,1:T(1,128)S(1)} %bitcast.3) | data formatting | bytes 128 | tf_op jit(solution)/shard_map/broadcast_in_dim | solution.py:336
  1.3 0.0 copy-start
  1.3 34.5 %shard_map.46 = f32[2,32,3072]{2,1,0:T(8,128)} custom-call(bf16[1,2,64,3072]{3,2,1,0:T(8,128)(2,1)} %slab_ref.1, f32[1,3072]{1,0:T(1,128)} %bitcast.2, s32[1,64,512]{2,1,0:T(8,128)} %density_ref.1, s32[16,1]{1,0:T(8,128)} %copy.5.offset_ref), custom_call_target="tpu_custom_call" | custom-call | tf_op jit(solution)/shard_map/pallas_call | solution.py:306
  35.8 0.0 copy-done
  35.8 2.1 %broadcast_multiply_fusion = f32[2,32,3072]{2,1,0:T(8,128)} fusion(f32[2,32,3072]{2,1,0:T(8,128)} %shard_map.46, f32[3072]{0:T(1024)S(1)} %broadcast_multiply_fusion.1), kind=kLoop, calls=%fused_computation | loop fusion | flops 196608 | bytes 1585152 | tf_op jit(solution)/shard_map/mul | solution.py:337
  (1 shorter events, 0.0 us)
Async XLA Ops:
  0.0 0.7 %copy-start.1 = (s32[16]{0:T(128)S(1)}, s32[16]{0:T(128)}, u32[]{:S(2)}) copy-start(s32[16]{0:T(128)} %param.7) | copy-start | bytes 196
  1.3 34.5 %copy-start = (f32[3072]{0:T(1024)S(1)}, f32[3072]{0:T(1024)}, u32[]{:S(2)}) copy-start(f32[3072]{0:T(1024)} %param.5) | copy-start | bytes 36868

commit v2 on v1

--- a/solution.py
+++ b/solution.py
@@ -41,44 +41,106 @@
     layers, facets, cols, width,
     slab_ref, window_ref, density_ref, offset_ref,
     out_ref,
-    wind, ca, sa, table, modulated, acc,
+    slab, counts_ref, window_here, offset_here, wind, ca, sa, table, modulated, acc,
     send1, recv1, embed, kr, ki, rr, ri, raw,
     send2, recv2,
-    ssem1, rsem1, ssem2, rsem2,
+    ssem1, rsem1, ssem2, rsem2, local_sem, up_sem, down_sem, layer_sem,
 ):
     layer = lax.axis_index("layer")
     me = lax.axis_index("facet")
-    rank = layer * facets + me
-    total = layers * facets
     image = facets * width
     groups = facets // GROUP
     part = cols // layers
+    mine = me // GROUP
+    half = mine // (groups // 2)
+    half_groups = groups // 2
+
+    def outward(step):
+        return jnp.where(
+            half == 0,
+            lax.rem(half_groups + step, groups),
+            lax.rem(half_groups - 1 - step + groups, groups),
+        )
+
+    def inward(step):
+        return jnp.where(half == 0, step, groups - 1 - step)
+
+    def signal(sem, where):
+        pl.semaphore_signal(sem, inc=1, device_id=where, device_id_type=MESH)
 
     barrier = pltpu.get_barrier_semaphore()
-
-    def greet(step, carry):
-        other = lax.rem(rank + step, total)
-        pl.semaphore_signal(
-            barrier, inc=1,
-            device_id=(other // facets, lax.rem(other, facets)), device_id_type=MESH,
-        )
-        return carry
-
-    lax.fori_loop(1, total, greet, 0)
-
-    window = window_ref[...]
-    for p in range(2):
-        wind[p * cols:(p + 1) * cols, :] = (
-            (slab_ref[0, p].astype(jnp.float32) * window).astype(jnp.bfloat16).astype(jnp.float32)
-        )
-
-    offs = offset_ref[...]
-    start = remainder(offs * me, facets) * width
-    cell = lax.broadcasted_iota(jnp.int32, (facets, width), 1)
-    turns = start + remainder(offs * cell, image)
-    cos_a, sin_a = sincos(turns, image)
-    ca[...] = cos_a
-    sa[...] = sin_a
+    for o in range(1, layers):
+        signal(barrier, (lax.rem(layer + o, layers), me))
+    for o in range(1, GROUP):
+        signal(barrier, (layer, mine * GROUP + lax.rem(me + o, GROUP)))
+    for o in range(GROUP):
+
+        @pl.when(mine > 0)
+        def _():
+            signal(barrier, (layer, (mine - 1) * GROUP + lax.rem(me + o, GROUP)))
+
+        @pl.when(mine < groups - 1)
+        def _():
+            signal(barrier, (layer, (mine + 1) * GROUP + lax.rem(me + o, GROUP)))
+
+    fetch_offsets = pltpu.make_async_copy(offset_ref, offset_here, local_sem.at[3])
+    fetch_offsets.start()
+    fetch_window = pltpu.make_async_copy(window_ref, window_here, local_sem.at[2])
+    fetch_window.start()
+    fetch_slab = pltpu.make_async_copy(slab_ref, slab, local_sem.at[0])
+    fetch_slab.start()
+    fetch_counts = pltpu.make_async_copy(density_ref, counts_ref, local_sem.at[1])
+    fetch_counts.start()
+
+    def relay(d, wanted_up, wanted_down):
+        has_up = mine + d <= groups - 1
+        has_down = mine - d >= 0
+
+        @pl.when(jnp.logical_and(has_up, wanted_up))
+        def _():
+            pl.semaphore_wait(up_sem.at[d], 1)
+            if d + 1 < groups:
+
+                @pl.when(mine > 0)
+                def _():
+                    signal(up_sem.at[d + 1], (layer, me - GROUP))
+
+        @pl.when(jnp.logical_and(has_down, wanted_down))
+        def _():
+            pl.semaphore_wait(down_sem.at[d], 1)
+            if d + 1 < groups:
+
+                @pl.when(mine < groups - 1)
+                def _():
+                    signal(down_sem.at[d + 1], (layer, me + GROUP))
+
+    first_up = jnp.where(half == 0, half_groups - mine, 1)
+    first_down = jnp.where(half == 1, mine - half_groups + 1, 1)
+
+    def meet_near():
+        @pl.when(mine == 0)
+        def _():
+            pl.semaphore_wait(barrier, 2 * GROUP - 1 + layers - 1)
+
+        @pl.when(mine == groups - 1)
+        def _():
+            pl.semaphore_wait(barrier, 2 * GROUP - 1 + layers - 1)
+
+        @pl.when(jnp.logical_and(mine > 0, mine < groups - 1))
+        def _():
+            pl.semaphore_wait(barrier, 3 * GROUP - 1 + layers - 1)
+            signal(up_sem.at[2], (layer, me - GROUP))
+            signal(down_sem.at[2], (layer, me + GROUP))
+
+        for d in range(2, groups):
+            relay(d, d <= first_up, d <= first_down)
+
+    def meet_far():
+        for d in range(2, groups):
+            relay(d, d > first_up, d > first_down)
+        for o in range(1, layers):
+            signal(layer_sem, (lax.rem(layer + o, layers), me))
+
 
     lane = lax.broadcasted_iota(jnp.int32, (ROWS, CONTRIB), 1) * STEP
     row = lax.broadcasted_iota(jnp.int32, (ROWS, CONTRIB), 0)
@@ -93,12 +155,31 @@
             base_c * rot_s + base_s * rot_c
         ).astype(jnp.bfloat16)
 
-    half = me // (facets // 2)
-    half_groups = groups // 2
+    fetch_offsets.wait()
+    square = (GROUP * groups, GROUP * groups)
+    on_diagonal = lax.broadcasted_iota(jnp.int32, square, 0) == lax.broadcasted_iota(jnp.int32, square, 1)
+    offs = jnp.sum(
+        jnp.where(on_diagonal, offset_here[...].astype(jnp.float32), 0.0), axis=1, keepdims=True
+    ).astype(jnp.int32)
+    start = remainder(offs * me, facets) * width
+    cell = lax.broadcasted_iota(jnp.int32, (facets, width), 1)
+    turns = start + remainder(offs * cell, image)
+    cos_a, sin_a = sincos(turns, image)
+    ca[...] = cos_a
+    sa[...] = sin_a
+
+    fetch_window.wait()
+    fetch_slab.wait()
+    window = window_here[...]
+    for p in range(2):
+        wind[p * cols:(p + 1) * cols, :] = (
+            (slab[0, p].astype(jnp.float32) * window).astype(jnp.bfloat16).astype(jnp.float32)
+        )
+
     scale1 = width ** -0.5
 
     def encode(step, carry):
-        g = lax.rem((1 - half) * half_groups + step, groups)
+        g = outward(step)
         for k in range(width // CHUNK):
             xs = slice(k * CHUNK, (k + 1) * CHUNK)
             for t in range(GROUP):
@@ -126,7 +207,11 @@
 
         @pl.when(step == 0)
         def _():
-            pl.semaphore_wait(barrier, total - 1)
+            meet_near()
+
+        @pl.when(step == 1)
+        def _():
+            meet_far()
 
         for t in range(GROUP):
             s = g * GROUP + t
@@ -175,7 +260,7 @@
     raw[...] = jnp.zeros_like(raw)
 
     def gather(step, carry):
-        g = lax.rem(half * half_groups + step, groups)
+        g = inward(step)
         for t in range(GROUP):
             f = g * GROUP + t
 
@@ -196,7 +281,8 @@
 
     lax.fori_loop(0, groups, gather, 0)
 
-    counts = density_ref[0]
+    fetch_counts.wait()
+    counts = counts_ref[0]
     weights = jnp.where(
         counts > 0, 1.0 / jnp.maximum(counts, 1).astype(jnp.float32), 0.0
     )
@@ -212,8 +298,10 @@
     )
     dims = (((1,), (1,)), ((), ()))
 
+    pl.semaphore_wait(layer_sem, layers - 1)
+
     def scatter(step, carry):
-        g = lax.rem((1 - half) * half_groups + step, groups)
+        g = outward(step)
         lo = pl.multiple_of(g * GROUP * CONTRIB, GROUP * CONTRIB)
         er = embed[pl.ds(lo, GROUP * CONTRIB), 0:SUB]
         ei = embed[pl.ds(lo, GROUP * CONTRIB), SUB:2 * SUB]
@@ -251,7 +339,7 @@
     out_ref[...] = jnp.zeros_like(out_ref)
 
     def adjoint(step, carry):
-        g = lax.rem(half * half_groups + step, groups)
+        g = inward(step)
         tops = []
         for t in range(GROUP):
             s = g * GROUP + t
@@ -306,9 +394,13 @@
     summed = pl.pallas_call(
         functools.partial(kernel, layers, facets, cols, width),
         out_shape=jax.ShapeDtypeStruct((2, part, width), f32),
-        in_specs=[pl.BlockSpec(memory_space=pltpu.VMEM)] * 4,
+        in_specs=[pl.BlockSpec(memory_space=pltpu.HBM)] * 4,
         out_specs=pl.BlockSpec(memory_space=pltpu.VMEM),
         scratch_shapes=[
+            pltpu.VMEM(slabs.shape, bf16),
+            pltpu.VMEM(density.shape, jnp.int32),
+            pltpu.VMEM((1, width), f32),
+            pltpu.VMEM((1, facets), jnp.int32),
             pltpu.VMEM((2 * cols, width), f32),
             pltpu.VMEM((facets, width), f32),
             pltpu.VMEM((facets, width), f32),
@@ -329,11 +421,15 @@
             pltpu.SemaphoreType.DMA((facets,)),
             pltpu.SemaphoreType.DMA((layers, facets)),
             pltpu.SemaphoreType.DMA((layers, facets)),
+            pltpu.SemaphoreType.DMA((4,)),
+            pltpu.SemaphoreType.REGULAR((facets // GROUP,)),
+            pltpu.SemaphoreType.REGULAR((facets // GROUP,)),
+            pltpu.SemaphoreType.REGULAR,
         ],
         compiler_params=pltpu.CompilerParams(
-            collective_id=0, has_side_effects=True, vmem_limit_bytes=56 * 1024 * 1024
+            collective_id=0, has_side_effects=True, vmem_limit_bytes=(14 + facets) * 1024 * 1024
         ),
-    )(slabs, window[None, :], density, offsets[:, None])
+    )(slabs, window[None, :], density, offsets[None, :])
     return summed * (window[None, None, :] * (facets * CONTRIB) ** -0.5)
 
 

time: 38.1 us -> 38 us (level)
  the two profiles are of different devices: /device:TPU:9 before, /device:TPU:1 now
where the time goes in v2:
time: 38 us; the launch traced here: 37.8 us
  Pallas kernels  34 us (89%)
  local copies, waits for them, and re-layouts  2.04 us (5%)
  other arithmetic  1.72 us (5%)
    pallas_call x1, Pallas kernels, shards(): pl.pallas_call(functools.partial(kernel, layers, facets, cols, width), ou...  34 us
    unnamed x8, local copies, waits for them, and re-layouts  2.04 us
    mul x2, other arithmetic, shards(): return summed * (window[None, None, :] * (facets * CONTRIB) ** (-0.5))  1.72 us

profile of v2, /device:TPU:1, one launch (start us, length us, event | category | flops | bytes accessed | tf_op | source)
XLA Modules:
  0.0 37.8 jit_solution(13859043737031827962)
XLA Ops:
  0.0 0.0 copy-start.2
  0.0 0.0 copy-start.3
  0.0 0.8 %broadcast_multiply_fusion.1 = f32[3072]{0:T(1024)S(1)} fusion(f32[3072]{0:T(1024)} %param.5), kind=kLoop, calls=%fused_computation.1 | loop fusion | flops 3072 | bytes 24576 | tf_op jit(solution)/shard_map/mul | solution.py:433
  0.8 0.0 copy-done.2
  0.8 0.0 copy-done.3
  0.8 0.0 copy-start
  0.8 1.1 %copy-done = bf16[1,2,64,3072]{3,2,1,0:T(8,128)(2,1)S(1)} copy-done((bf16[1,2,64,3072]{3,2,1,0:T(8,128)(2,1)S(1)}, bf16[1,2,64,3072]{3,2,1,0:T(8,128)(2,1)}, u32[]{:S(2)}) %copy-start) | copy-done | bytes 786456
  1.9 0.0 copy-start.1
  1.9 0.9 %copy-done.1 = s32[1,64,512]{2,1,0:T(8,128)S(1)} copy-done((s32[1,64,512]{2,1,0:T(8,128)S(1)}, s32[1,64,512]{2,1,0:T(8,128)}, u32[]{:S(2)}) %copy-start.1) | copy-done | bytes 131096
  2.8 34.0 %shard_map.46 = f32[2,32,3072]{2,1,0:T(8,128)S(1)} custom-call(bf16[1,2,64,3072]{3,2,1,0:T(8,128)(2,1)S(1)} %copy-done, f32[1,3072]{1,0:T(1,128)S(1)} %bitcast.2, s32[1,64,512]{2,1,0:T(8,128)S(1)} %copy-done.1, s32[1,16]{1,0:T(1,128)S(1)} %bitcast.3), custom_call_target="tpu_custom_call" | custom-call | tf_op jit(solution)/shard_map/pallas_call | solution.py:394
  36.8 0.9 %broadcast_multiply_fusion = f32[2,32,3072]{2,1,0:T(8,128)} fusion(f32[2,32,3072]{2,1,0:T(8,128)S(1)} %shard_map.46, f32[3072]{0:T(1024)S(1)} %broadcast_multiply_fusion.1), kind=kLoop, calls=%fused_computation | loop fusion | flops 196608 | bytes 1585152 | tf_op jit(solution)/shard_map/mul | solution.py:433
Async XLA Ops:
  0.0 0.8 %copy-start.2 = (f32[3072]{0:T(1024)S(1)}, f32[3072]{0:T(1024)}, u32[]{:S(2)}) copy-start(f32[3072]{0:T(1024)} %param.5) | copy-start | bytes 36868
  0.0 0.8 %copy-start.3 = (s32[16]{0:T(128)S(1)}, s32[16]{0:T(128)}, u32[]{:S(2)}) copy-start(s32[16]{0:T(128)} %param.7) | copy-start | bytes 196
  0.8 1.1 %copy-start = (bf16[1,2,64,3072]{3,2,1,0:T(8,128)(2,1)S(1)}, bf16[1,2,64,3072]{3,2,1,0:T(8,128)(2,1)}, u32[]{:S(2)}) copy-start(bf16[1,2,64,3072]{3,2,1,0:T(8,128)(2,1)} %slab_ref.1) | copy-start | bytes 2359300
  1.9 0.9 %copy-start.1 = (s32[1,64,512]{2,1,0:T(8,128)S(1)}, s32[1,64,512]{2,1,0:T(8,128)}, u32[]{:S(2)}) copy-start(s32[1,64,512]{2,1,0:T(8,128)} %density_ref.1) | copy-start | bytes 393220

commit v3 on v2

--- a/solution.py
+++ b/solution.py
@@ -429,8 +429,13 @@
         compiler_params=pltpu.CompilerParams(
             collective_id=0, has_side_effects=True, vmem_limit_bytes=(14 + facets) * 1024 * 1024
         ),
-    )(slabs, window[None, :], density, offsets[None, :])
-    return summed * (window[None, None, :] * (facets * CONTRIB) ** -0.5)
+    )(
+        *(
+            pltpu.with_memory_space_constraint(x, pltpu.HBM)
+            for x in (slabs, window[None, :], density, offsets[None, :])
+        )
+    )
+    return summed * (facets * CONTRIB) ** -0.5 * window[None, None, :]
 
 
 def solution(mesh):

time: 38 us -> 35.8 us (0.942)
  local copies, waits for them, and re-layouts: 2.04 us -> 0 us
    unnamed x8 -> x0, local copies, waits for them, and re-layouts: 2.04 us -> none
where the time goes in v3:
time: 35.8 us; the launch traced here: 35.5 us
  Pallas kernels  33.9 us (95%)
  other arithmetic  1.65 us (5%)
    pallas_call x1, Pallas kernels, shards(): pl.pallas_call(functools.partial(kernel, layers, facets, cols, width), ou...  33.9 us
    mul x2, other arithmetic, shards(): return summed * (facets * CONTRIB) ** (-0.5) * window[None, None, :]  1.65 us

profile of v3, /device:TPU:1, one launch (start us, length us, event | category | flops | bytes accessed | tf_op | source)
XLA Modules:
  0.0 35.5 jit_solution(11930982137575732235)
XLA Ops:
  0.0 0.7 %broadcast_multiply_fusion.1 = f32[3072]{0:T(1024)S(1)} fusion(f32[3072]{0:T(1024)} %param.5), kind=kLoop, calls=%fused_computation.1 | loop fusion | flops 3072 | bytes 24576 | tf_op jit(solution)/shard_map/mul | solution.py:438
  0.7 33.9 %shard_map.46 = f32[2,32,3072]{2,1,0:T(8,128)S(1)} custom-call(bf16[1,2,64,3072]{3,2,1,0:T(8,128)(2,1)} %slab_ref.1, f32[1,3072]{1,0:T(1,128)} %bitcast.2, s32[1,64,512]{2,1,0:T(8,128)} %density_ref.1, s32[1,16]{1,0:T(1,128)} %bitcast.3), custom_call_target="tpu_custom_call" | custom-call | tf_op jit(solution)/shard_map/pallas_call | solution.py:394
  34.6 0.9 %broadcast_multiply_fusion = f32[2,32,3072]{2,1,0:T(8,128)} fusion(f32[2,32,3072]{2,1,0:T(8,128)S(1)} %shard_map.46, f32[3072]{0:T(1024)S(1)} %broadcast_multiply_fusion.1), kind=kLoop, calls=%fused_computation | loop fusion | flops 196608 | bytes 1585152 | tf_op jit(solution)/shard_map/mul | solution.py:438

commit v4 on v3

--- a/solution.py
+++ b/solution.py
@@ -337,6 +337,7 @@
     lax.fori_loop(0, groups, scatter, 0)
 
     out_ref[...] = jnp.zeros_like(out_ref)
+    out_scale = (facets * CONTRIB) ** -0.5
 
     def adjoint(step, carry):
         g = inward(step)
@@ -377,8 +378,9 @@
                 gi = prod[(2 * t + 1) * part:(2 * t + 2) * part]
                 out_r = out_r + (c_row * gr - s_row * gi)
                 out_i = out_i + (c_row * gi + s_row * gr)
-            out_ref[0, :, xs] = out_r
-            out_ref[1, :, xs] = out_i
+            factor = jnp.where(step == groups - 1, window_here[:, xs] * out_scale, 1.0)
+            out_ref[0, :, xs] = out_r * factor
+            out_ref[1, :, xs] = out_i * factor
         return carry
 
     lax.fori_loop(0, groups, adjoint, 0)
@@ -435,7 +437,7 @@
             for x in (slabs, window[None, :], density, offsets[None, :])
         )
     )
-    return summed * (facets * CONTRIB) ** -0.5 * window[None, None, :]
+    return summed
 
 
 def solution(mesh):

time: 35.8 us -> 35.1 us (0.980)
  other arithmetic: 1.65 us -> 0 us
  local copies, waits for them, and re-layouts: 0 us -> 0.88 us
    mul x2 -> x0, other arithmetic: 1.65 us -> none  [shards(): return summed * (facets * CONTRIB) ** (-0.5) * window[None, None, :]]
    unnamed x0 -> x1, local copies, waits for them, and re-layouts: none -> 0.88 us
where the time goes in v4:
time: 35.1 us; the launch traced here: 35 us
  Pallas kernels  34.1 us (97%)
  local copies, waits for them, and re-layouts  0.88 us (3%)
    pallas_call x1, Pallas kernels, shards(): pl.pallas_call(functools.partial(kernel, layers, facets, cols, width), ou...  34.1 us
    unnamed x1, local copies, waits for them, and re-layouts  0.88 us

profile of v4, /device:TPU:1, one launch (start us, length us, event | category | flops | bytes accessed | tf_op | source)
XLA Modules:
  0.0 35.0 jit_solution(17539739321278223189)
XLA Ops:
  0.0 34.1 %shard_map.46 = f32[2,32,3072]{2,1,0:T(8,128)S(1)} custom-call(bf16[1,2,64,3072]{3,2,1,0:T(8,128)(2,1)} %slab_ref.1, f32[1,3072]{1,0:T(1,128)} %bitcast.2, s32[1,64,512]{2,1,0:T(8,128)} %density_ref.1, s32[1,16]{1,0:T(1,128)} %bitcast.3), custom_call_target="tpu_custom_call" | custom-call | tf_op jit(solution)/shard_map/pallas_call | solution.py:396
  34.1 0.9 %copy.6 = f32[2,32,3072]{2,1,0:T(8,128)} copy(f32[2,32,3072]{2,1,0:T(8,128)S(1)} %shard_map.46) | data formatting | bytes 1572864

commit v5 on v4

--- a/solution.py
+++ b/solution.py
@@ -11,6 +11,8 @@
 CONTRIB = 128
 SUB = 512
 GROUP = 4
+PIECE = 2
+PIECES = GROUP // PIECE
 CHUNK = 512
 ROWS = 256
 STEP = SUB // CONTRIB
@@ -260,9 +262,9 @@
     raw[...] = jnp.zeros_like(raw)
 
     def gather(step, carry):
-        g = inward(step)
-        for t in range(GROUP):
-            f = g * GROUP + t
+        first = inward(step // PIECES) * GROUP + lax.rem(step, PIECES) * PIECE
+        for t in range(PIECE):
+            f = first + t
 
             @pl.when(f != me)
             def _():
@@ -272,14 +274,14 @@
                     device_id=(layer, f), device_id_type=MESH,
                 ).wait()
 
-        lhs = jnp.concatenate([recv1[g * GROUP + t] for t in range(GROUP)], axis=1)
-        lo = pl.multiple_of(g * GROUP * CONTRIB, GROUP * CONTRIB)
+        lhs = jnp.concatenate([recv1[first + t] for t in range(PIECE)], axis=1)
+        lo = pl.multiple_of(first * CONTRIB, PIECE * CONTRIB)
         raw[...] += jnp.dot(
-            lhs, embed[pl.ds(lo, GROUP * CONTRIB), :], preferred_element_type=jnp.float32
+            lhs, embed[pl.ds(lo, PIECE * CONTRIB), :], preferred_element_type=jnp.float32
         )
         return carry
 
-    lax.fori_loop(0, groups, gather, 0)
+    lax.fori_loop(0, groups * PIECES, gather, 0)
 
     fetch_counts.wait()
     counts = counts_ref[0]
@@ -301,22 +303,22 @@
     pl.semaphore_wait(layer_sem, layers - 1)
 
     def scatter(step, carry):
-        g = outward(step)
-        lo = pl.multiple_of(g * GROUP * CONTRIB, GROUP * CONTRIB)
-        er = embed[pl.ds(lo, GROUP * CONTRIB), 0:SUB]
-        ei = embed[pl.ds(lo, GROUP * CONTRIB), SUB:2 * SUB]
+        first = outward(step // PIECES) * GROUP + lax.rem(step, PIECES) * PIECE
+        lo = pl.multiple_of(first * CONTRIB, PIECE * CONTRIB)
+        er = embed[pl.ds(lo, PIECE * CONTRIB), 0:SUB]
+        ei = embed[pl.ds(lo, PIECE * CONTRIB), SUB:2 * SUB]
         pr = lax.dot_general(gridded, er, dims, preferred_element_type=jnp.float32)
         pi = lax.dot_general(gridded, ei, dims, preferred_element_type=jnp.float32)
         real = ((pr[0:cols] + pi[cols:2 * cols]) * 0.5).astype(jnp.bfloat16)
         imag = ((pr[cols:2 * cols] - pi[0:cols]) * 0.5).astype(jnp.bfloat16)
-        for t in range(GROUP):
-            f = g * GROUP + t
+        for t in range(PIECE):
+            f = first + t
             js = slice(t * CONTRIB, (t + 1) * CONTRIB)
             for l in range(layers):
                 send2[f, l, 0] = real[l * part:(l + 1) * part, js]
                 send2[f, l, 1] = imag[l * part:(l + 1) * part, js]
-        for t in range(GROUP):
-            f = g * GROUP + t
+        for t in range(PIECE):
+            f = first + t
             for l in range(layers):
                 own = jnp.logical_and(f == me, layer == l)
 
@@ -334,7 +336,7 @@
 
         return carry
 
-    lax.fori_loop(0, groups, scatter, 0)
+    lax.fori_loop(0, groups * PIECES, scatter, 0)
 
     out_ref[...] = jnp.zeros_like(out_ref)
     out_scale = (facets * CONTRIB) ** -0.5

time: 35.1 us -> 35.6 us (1.014)
  Pallas kernels: 34.1 us -> 34.5 us
    pallas_call x1, Pallas kernels: 34.1 us -> 34.5 us  [shards(): pl.pallas_call(functools.partial(kernel, layers, facets, cols, width), ou...]
where the time goes in v5:
time: 35.6 us; the launch traced here: 35.4 us
  Pallas kernels  34.5 us (97%)
  local copies, waits for them, and re-layouts  0.88 us (2%)
    pallas_call x1, Pallas kernels, shards(): pl.pallas_call(functools.partial(kernel, layers, facets, cols, width), ou...  34.5 us
    unnamed x1, local copies, waits for them, and re-layouts  0.88 us

profile of v5, /device:TPU:1, one launch (start us, length us, event | category | flops | bytes accessed | tf_op | source)
XLA Modules:
  0.0 35.4 jit_solution(13620959480968861304)
XLA Ops:
  0.0 34.5 %shard_map.46 = f32[2,32,3072]{2,1,0:T(8,128)S(1)} custom-call(bf16[1,2,64,3072]{3,2,1,0:T(8,128)(2,1)} %slab_ref.1, f32[1,3072]{1,0:T(1,128)} %bitcast.2, s32[1,64,512]{2,1,0:T(8,128)} %density_ref.1, s32[1,16]{1,0:T(1,128)} %bitcast.3), custom_call_target="tpu_custom_call" | custom-call | tf_op jit(solution)/shard_map/pallas_call | solution.py:398
  34.5 0.9 %copy.6 = f32[2,32,3072]{2,1,0:T(8,128)} copy(f32[2,32,3072]{2,1,0:T(8,128)S(1)} %shard_map.46) | data formatting | bytes 1572864
